TPU v7x, 32 devices: a whole 2x2x4 slice. The times are simulated.
32 devices in a mesh: groups: 1, ctx: 16 (over z, y, x), tp: 2 (over core).
Axes of the slice: x: 2, y: 2, z: 4, core: 2. Of those that a mesh axis runs over, the one named last changes fastest.
Arguments:
- queries: bfloat16 [4, 32, 64, 128], P('groups', 'ctx', 'tp'), may hold values from -100 to 100
- cand_keys: bfloat16 [4, 32, 8, 128], P('groups', 'ctx', 'tp'), may hold values from -4 to 4
- candidate_values: bfloat16 [4, 32, 8, 128], P('groups', 'ctx', 'tp'), may hold values from -5 to 5
- cached_prompt_keys: bfloat16 [256, 128, 8, 128], P(('groups', 'ctx'), None, 'tp'), may hold values from -4 to 4
- cached_prompt_values: bfloat16 [256, 128, 8, 128], P(('groups', 'ctx'), None, 'tp'), may hold values from -5 to 5
- block_lists: int32 [4, 128], P('groups'), may hold values from 0 to 255, as said below
- out_weight: bfloat16 [8192, 8192], P('tp', 'ctx'), may hold values from -0.0625 to 0.0625
Outputs:
- verified: bfloat16 [4, 32, 8192], P('groups', 'tp', 'ctx')
Inputs may be any that keep to these rules, and one draw needn't show every extreme that they name: `block_lists`: each row holds 128 distinct block numbers in increasing order; among blocks 16 * c to 16 * (c + 1) - 1 a row has at most 16 entries, exactly 16 for some c in every row; all rows together have at most 40 entries in one such range, exactly 40 in some.
All inputs are finite; a program needn't handle non-finite values.
Results may differ from a plain program's by a relative error of at most 0.022.
Values may be sent and summed in bfloat16 or wider, within the bound.
A program may use at most 128 MiB of HBM per device.

v0:
```python
import jax
import jax.numpy as jnp
from jax import lax
from jax.sharding import PartitionSpec as P

NEGATIVE = -1e30


def masked_softmax(scores, visible):
    scores = jnp.where(visible, scores, NEGATIVE)
    maxima = jnp.max(scores, axis=-1)
    weights = jnp.where(visible, jnp.exp(scores - maxima[..., None]), 0.0)
    return (weights, maxima, jnp.sum(weights, axis=-1))


def heads_last(stats):
    kv_count, query_group_width, row_count = stats.shape
    return jnp.transpose(stats, (2, 0, 1)).reshape(row_count, kv_count * query_group_width)


def block_terms(query_matrix, block_keys, block_values, visible, factor):
    row_count, kv_count, query_group_width, head_size = query_matrix.shape
    scores = (
        jnp.einsum("nkgd,mkd->kgnm", query_matrix, block_keys, preferred_element_type=jnp.float32)
        * factor
    )
    weights, maxima, denominator = masked_softmax(scores, visible)
    numerator = jnp.einsum(
        "kgnm,mkd->nkgd",
        weights.astype(jnp.bfloat16),
        block_values,
        preferred_element_type=jnp.float32,
    )
    return (
        numerator.reshape(row_count, kv_count * query_group_width, head_size),
        heads_last(maxima),
        heads_last(denominator),
    )


def join_parts(first, second):
    maxima = jnp.maximum(first[1], second[1])
    left_scale = jnp.exp(first[1] - maxima)
    right_scale = jnp.exp(second[1] - maxima)
    numerator = first[0] * left_scale[..., None] + second[0] * right_scale[..., None]
    return (numerator, maxima, first[2] * left_scale + second[2] * right_scale)


def sources_merge(parts):
    numerator, maxima, denominator = parts
    highest = jnp.max(maxima, axis=2)
    rescale = jnp.exp(maxima - highest[:, :, None])
    return (
        jnp.sum(numerator * rescale[..., None], axis=2),
        highest,
        jnp.sum(denominator * rescale, axis=2),
    )


def on_device(
    queries,
    cand_keys,
    candidate_values,
    cached_prompt_keys,
    cached_prompt_values,
    block_lists,
    out_weight,
):
    cand_count, tok_rows, head_local, head_size = queries.shape
    kv_local = cand_keys.shape[2]
    query_group_width = head_local // kv_local
    blocks_here, block_tokens = (cached_prompt_keys.shape[0], cached_prompt_keys.shape[1])
    selected = block_lists.shape[1]
    ranges = lax.axis_size("ctx")
    device = lax.axis_index("ctx")
    cand_length = tok_rows * ranges
    factor = head_size ** (-0.5)
    capacity = min(blocks_here, 4 * selected // ranges)
    lowest = device * blocks_here
    below = jnp.sum((block_lists < lowest).astype(jnp.int32), axis=1)
    inside = jnp.sum((block_lists < lowest + blocks_here).astype(jnp.int32), axis=1) - below
    slot_ids = jnp.arange(capacity)
    where_listed = jnp.clip(below[:, None] + slot_ids[None, :], 0, selected - 1)
    slot_live = slot_ids[None, :] < inside[:, None]
    local_index = jnp.where(
        slot_live, jnp.take_along_axis(block_lists, where_listed, axis=1) - lowest, 0
    )
    gathered_keys = jnp.take(cached_prompt_keys, local_index, axis=0).reshape(
        cand_count, capacity * block_tokens, kv_local, head_size
    )
    gathered_values = jnp.take(cached_prompt_values, local_index, axis=0).reshape(
        cand_count, capacity * block_tokens, kv_local, head_size
    )
    key_live = jnp.repeat(slot_live, block_tokens, axis=1)
    shard_rows = lax.all_gather(queries, "ctx", axis=1, tiled=True)
    row_count = shard_rows.shape[1]
    grouped_queries = shard_rows.reshape(
        cand_count, row_count, kv_local, query_group_width, head_size
    )
    terms = lax.map(
        lambda parts: block_terms(parts[0], parts[1], parts[2], parts[3], factor),
        (grouped_queries, gathered_keys, gathered_values, key_live),
    )
    prompt_parts = tuple((fresh for fresh in terms))
    candidate_own_keys, own_values = (
        lax.all_gather(cand_keys, "ctx", axis=1, tiled=True),
        lax.all_gather(candidate_values, "ctx", axis=1, tiled=True),
    )
    query_pos = device * tok_rows + jnp.arange(tok_rows)
    causal = jnp.arange(cand_length)[None, :] <= query_pos[:, None]
    grouped_local = queries.reshape(cand_count, tok_rows, kv_local, query_group_width, head_size)
    own_scores = (
        jnp.einsum(
            "jnkgd,jmkd->jkgnm",
            grouped_local,
            candidate_own_keys,
            preferred_element_type=jnp.float32,
        )
        * factor
    )
    own_weights, own_max, own_sum = masked_softmax(own_scores, causal)
    own_numer = jnp.einsum(
        "jkgnm,jmkd->jnkgd",
        own_weights.astype(jnp.bfloat16),
        own_values,
        preferred_element_type=jnp.float32,
    )
    own_part = (
        own_numer.reshape(cand_count, tok_rows, head_local, head_size),
        jnp.transpose(own_max, (0, 3, 1, 2)).reshape(cand_count, tok_rows, head_local),
        jnp.transpose(own_sum, (0, 3, 1, 2)).reshape(cand_count, tok_rows, head_local),
    )
    merged = sources_merge(
        (
            lax.all_to_all(
                prompt_parts[0][:, :, None].astype(jnp.bfloat16),
                "ctx",
                split_axis=1,
                concat_axis=2,
                tiled=True,
            ).astype(jnp.float32),
            lax.all_to_all(
                prompt_parts[1][:, :, None].astype(jnp.bfloat16),
                "ctx",
                split_axis=1,
                concat_axis=2,
                tiled=True,
            ).astype(jnp.float32),
            lax.all_to_all(
                prompt_parts[2][:, :, None].astype(jnp.bfloat16),
                "ctx",
                split_axis=1,
                concat_axis=2,
                tiled=True,
            ).astype(jnp.float32),
        )
    )
    numerator, unused_max, denominator = join_parts(merged, own_part)
    attention = (
        (numerator / denominator[..., None])
        .reshape(cand_count, tok_rows, head_local * head_size)
        .astype(jnp.bfloat16)
    )
    partial_value = jnp.einsum(
        "jnf,fc->jnc",
        lax.all_gather(attention, "ctx", axis=1, tiled=True),
        out_weight,
        preferred_element_type=jnp.float32,
    )
    return lax.psum_scatter(
        partial_value.astype(jnp.bfloat16), "tp", scatter_dimension=1, tiled=True
    )


def solution(mesh):
    placed = (
        P("groups", "ctx", "tp", None),
        P("groups", "ctx", "tp", None),
        P("groups", "ctx", "tp", None),
        P(("groups", "ctx"), None, "tp", None),
        P(("groups", "ctx"), None, "tp", None),
        P("groups", None),
        P("tp", "ctx"),
    )
    return jax.shard_map(
        on_device, mesh=mesh, in_specs=placed, out_specs=P("groups", "tp", "ctx"), check_vma=False
    )
```

profile of v0, /device:TPU:0, one launch (start us, length us, event | category | flops | bytes accessed | tf_op | source)
XLA Modules:
  0.0 323.0 jit_solution(12083824224312323788)
XLA Ops:
  10.1 9.3 %gather_fusion.1 = bf16[64,128,4,128]{3,2,1,0:T(4,128)(2,1)} fusion(bf16[16,128,4,128]{3,2,1,0:T(4,128)(2,1)S(1)} %copy-done, s32[1024]{0:T(1024)S(1)} %pad_clamp_fusion), kind=kCustom, calls=%fused_computation.clone | custom fusion | bytes 16777472 | tf_op jit(solution)/shard_map/jit(_take)/gather | solution.py:91
  19.4 10.9 %gather_fusion.2 = bf16[64,128,4,128]{3,2,1,0:T(4,128)(2,1)} fusion(bf16[16,128,4,128]{3,2,1,0:T(4,128)(2,1)} %param.14, s32[1024]{0:T(1024)S(1)} %pad_clamp_fusion), kind=kCustom, calls=%fused_computation.1.clone | custom fusion | bytes 16777472 | tf_op jit(solution)/shard_map/jit(_take)/gather | solution.py:88
  30.5 14.7 %copy_select_fusion = (bf16[4,16,128,4,128]{4,2,1,3,0:T(8,128)(2,1)}, bf16[4,16,128,4,128]{4,2,1,3,0:T(8,128)(2,1)}) fusion(bf16[4,16,128,4,128]{4,3,2,1,0:T(4,128)(2,1)} %bitcast.150, pred[4,16]{1,0:T(4,128)(4,1)S(1)} %get-tuple-element.82, bf16[4,16,128,4,128]{4,3,2,1,0:T(4,128)(2,1)} %bitcast.149), kind=kLoop, calls=%fused_computation.27 | loop fusion | flops 8388608 | bytes 33554496 | tf_op jit(solution)/shard_map/jit(_take)/select_n | solution.py:88
  45.1 22.6 %all-gather.3.cloned.1.call-done = bf16[4,32,32,128]{3,2,1,0:T(8,128)(2,1)} async-done(((bf16[4,2,32,128]{3,2,1,0:T(8,128)(2,1)}), bf16[4,32,32,128]{3,2,1,0:T(8,128)(2,1)}) %all-gather.3.cloned.1.call-update) | async-done | bytes 1048592 | tf_op jit(solution)/shard_map/all_gather | solution.py:95
  69.4 61.6 %while.14 = (s32[]{:T(128)}, bf16[4,32,32,128]{3,2,0,1:T(8,128)(2,1)}, bf16[4,32,32]{2,0,1:T(4,128)(2,1)S(1)}, bf16[4,32,32]{2,0,1:T(4,128)(2,1)S(1)}, bf16[4,20...) while((s32[]{:T(128)}, ...), condition=%wide.region_5.7_spmd, body=%wide.region_2.6_spmd.sunk | while | flops 1101002752 | bytes 64022668 | solution.py:100
  72.5 3.2 copy-done.1
  78.1 5.7 %fusion.58 = bf16[4,128,8,32]{1,3,2,0:T(8,128)(2,1)S(1)} fusion(f32[4,2048,32,8]{1,2,3,0:T(8,128)} %copy-done.1, f32[4,8,32]{2,1,0:T(8,128)S(1)} %get-tuple-element.148, pred[2048]{0:T(1024)(128)(4,1)S(1)} %dynamic-slice_reduce_fusion.2, bf16[4,2048,4,128]{3,1,2,0:T(8,128)(2,1)} %get-tuple-element.173, s32[]{:T(128)} %get-tuple-element.159), kind=kOutput, calls=%fused_computation.10.clone.1 | convolution fusion | flops 547356672 | bytes 10768896 | tf_op jit(solution)/shard_map/while/body/eval_jaxpr/kgnm,mkd->nkgd/dot_general | solution.py:28
  87.9 3.2 copy-done.1
  93.5 5.7 %fusion.58 = bf16[4,128,8,32]{1,3,2,0:T(8,128)(2,1)S(1)} fusion(f32[4,2048,32,8]{1,2,3,0:T(8,128)} %copy-done.1, f32[4,8,32]{2,1,0:T(8,128)S(1)} %get-tuple-element.148, pred[2048]{0:T(1024)(128)(4,1)S(1)} %dynamic-slice_reduce_fusion.2, bf16[4,2048,4,128]{3,1,2,0:T(8,128)(2,1)} %get-tuple-element.173, s32[]{:T(128)} %get-tuple-element.159), kind=kOutput, calls=%fused_computation.10.clone.1 | convolution fusion | flops 547356672 | bytes 10768896 | tf_op jit(solution)/shard_map/while/body/eval_jaxpr/kgnm,mkd->nkgd/dot_general | solution.py:28
  103.3 3.2 copy-done.1
  108.9 5.7 %fusion.58 = bf16[4,128,8,32]{1,3,2,0:T(8,128)(2,1)S(1)} fusion(f32[4,2048,32,8]{1,2,3,0:T(8,128)} %copy-done.1, f32[4,8,32]{2,1,0:T(8,128)S(1)} %get-tuple-element.148, pred[2048]{0:T(1024)(128)(4,1)S(1)} %dynamic-slice_reduce_fusion.2, bf16[4,2048,4,128]{3,1,2,0:T(8,128)(2,1)} %get-tuple-element.173, s32[]{:T(128)} %get-tuple-element.159), kind=kOutput, calls=%fused_computation.10.clone.1 | convolution fusion | flops 547356672 | bytes 10768896 | tf_op jit(solution)/shard_map/while/body/eval_jaxpr/kgnm,mkd->nkgd/dot_general | solution.py:28
  115.7 3.0 bitcast_reduce_fusion.2
  118.7 3.2 copy-done.1
  124.3 5.7 %fusion.58 = bf16[4,128,8,32]{1,3,2,0:T(8,128)(2,1)S(1)} fusion(f32[4,2048,32,8]{1,2,3,0:T(8,128)} %copy-done.1, f32[4,8,32]{2,1,0:T(8,128)S(1)} %get-tuple-element.148, pred[2048]{0:T(1024)(128)(4,1)S(1)} %dynamic-slice_reduce_fusion.2, bf16[4,2048,4,128]{3,1,2,0:T(8,128)(2,1)} %get-tuple-element.173, s32[]{:T(128)} %get-tuple-element.159), kind=kOutput, calls=%fused_computation.10.clone.1 | convolution fusion | flops 547356672 | bytes 10768896 | tf_op jit(solution)/shard_map/while/body/eval_jaxpr/kgnm,mkd->nkgd/dot_general | solution.py:28
  131.8 4.5 %all-to-all-start.2 = ((bf16[16,2,128]{2,1,0:T(2,128)(2,1)}), bf16[16,2,128]{2,1,0:T(2,128)(2,1)S(1)}, u32[]{:S(2)}, u32[]{:S(2)}) async-start(bf16[16,2,128]{2,1,0:T(2,128)(2,1)} %reshape.228), calls=%async_computation.2 | async-start | bytes 16384 | tf_op jit(solution)/shard_map/all_to_all | solution.py:149
  136.4 7.1 %all-to-all-done.2 = bf16[16,2,128]{2,1,0:T(2,128)(2,1)S(1)} async-done(((bf16[16,2,128]{2,1,0:T(2,128)(2,1)}), bf16[16,2,128]{2,1,0:T(2,128)(2,1)S(1)}, u32[]{:S(2)}, u32[]{:S(2)}) %all-to-all-start.2) | async-done | bytes 8224 | tf_op jit(solution)/shard_map/all_to_all | solution.py:149
  143.5 9.9 %all_to_all.33 = bf16[16,2,128]{2,1,0:T(2,128)(2,1)S(1)} all-to-all(bf16[16,2,128]{2,1,0:T(2,128)(2,1)S(1)} %reshape.226), channel_id=1, replica_groups=mesh['groups'=1,'ctx'=16,'tp'=2] {'ctx'}, dimensions={0} | all-to-all | bytes 16384 | tf_op jit(solution)/shard_map/all_to_all | solution.py:142
  153.4 3.7 %all-to-all-start = ((bf16[4,32,1,32,128]{4,3,0,2,1:T(8,128)(2,1)}), bf16[4,32,1,32,128]{4,3,0,2,1:T(8,128)(2,1)S(1)}, u32[]{:S(2)}, u32[]{:S(2)}) async-start(bf16[4,32,1,32,128]{4,3,0,2,1:T(8,128)(2,1)} %bitcast.156), calls=%async_computation | async-start | bytes 2097152 | tf_op jit(solution)/shard_map/all_to_all | solution.py:135
  157.1 47.7 %all_gather.13 = bf16[4,32,4,128]{3,2,0,1:T(4,128)(2,1)S(1)} all-gather(bf16[4,2,4,128]{3,2,0,1:T(4,128)(2,1)S(1)} %copy.77), channel_id=1, replica_groups=mesh['groups'=1,'ctx'=16,'tp'=2] {'ctx'}, dimensions={1}, use_global_device_ids=true | all-gather | bytes 139264 | tf_op jit(solution)/shard_map/all_gather | solution.py:106
  205.6 38.1 %all_gather.14 = bf16[4,32,4,128]{3,2,0,1:T(4,128)(2,1)S(1)} all-gather(bf16[4,2,4,128]{3,2,0,1:T(4,128)(2,1)S(1)} %copy.82), channel_id=1, replica_groups=mesh['groups'=1,'ctx'=16,'tp'=2] {'ctx'}, dimensions={1}, use_global_device_ids=true | all-gather | bytes 139264 | tf_op jit(solution)/shard_map/all_gather | solution.py:107
  248.7 3.9 %fusion.22 = f32[4,2,32,128]{3,1,2,0:T(2,128)S(1)} fusion(f32[4,16,2,1,32,128]{5,4,0,2,1,3:T(8,128)S(1)} %convert.23, f32[4,2,16,32]{1,2,3,0:T(8,128)} %copy.76), kind=kLoop, calls=%fused_computation.32 | loop fusion | flops 1015808 | bytes 2244608 | tf_op jit(solution)/shard_map/reduce_sum | solution.py:54
  254.4 51.1 %all-gather.5.cloned.1.call-done = bf16[4,32,4096]{2,0,1:T(4,128)(2,1)} async-done(((bf16[4,2,4096]{2,0,1:T(4,128)(2,1)}), bf16[4,32,4096]{2,0,1:T(4,128)(2,1)}) %all-gather.5.cloned.1.call-update) | async-done | bytes 1048592 | tf_op jit(solution)/shard_map/all_gather | solution.py:166
  305.5 4.4 %fusion.23 = bf16[4,32,512]{2,1,0:T(8,128)(2,1)} fusion(bf16[4096,512]{1,0:T(8,128)(2,1)} %param.17, bf16[4,32,4096]{2,0,1:T(4,128)(2,1)} %all-gather.5.cloned.1.call-done), kind=kOutput, calls=%fused_computation.33 | convolution fusion | flops 536936448 | bytes 5373952 | tf_op jit(solution)/shard_map/jnf,fc->jnc/dot_general | solution.py:164
  309.9 6.6 %reduce-scatter.2.cloned.1.call-done = bf16[4,16,512]{2,1,0:T(8,128)(2,1)} async-done(((bf16[4,32,512]{2,1,0:T(8,128)(2,1)}), bf16[4,16,512]{2,1,0:T(8,128)(2,1)}) %reduce-scatter.2.cloned.1.call-update) | async-done | bytes 65552 | tf_op jit(solution)/shard_map/reduce_scatter | solution.py:170
  (99 shorter events, 36.4 us)
Async XLA Ops:
  6.5 3.6 %copy-start = (bf16[16,128,4,128]{3,2,1,0:T(4,128)(2,1)S(1)}, bf16[16,128,4,128]{3,2,1,0:T(4,128)(2,1)}, u32[]{:S(2)}) copy-start(bf16[16,128,4,128]{3,2,1,0:T(4,128)(2,1)} %param.15) | copy-start | bytes 6291460
  6.5 61.2 %all-gather.3.cloned.1.call-start = ((), (), s32[]{:S(2)}) async-start(), calls=%async_computation.4 | async-start | bytes 1114112 | tf_op jit(solution)/shard_map/all_gather | solution.py:95
  69.4 87.7 %copy-start.3 = (bf16[4,2,4,128]{3,2,1,0:T(4,128)(2,1)S(1)}, bf16[4,2,4,128]{3,2,1,0:T(4,128)(2,1)}, u32[]{:S(2)}) copy-start(bf16[4,2,4,128]{3,2,1,0:T(4,128)(2,1)} %param.12) | copy-start | bytes 24580
  69.4 135.4 %copy-start.2 = (bf16[4,2,32,128]{3,2,1,0:T(8,128)(2,1)S(1)}, bf16[4,2,32,128]{3,2,1,0:T(8,128)(2,1)}, u32[]{:S(2)}) copy-start(bf16[4,2,32,128]{3,2,1,0:T(8,128)(2,1)} %param.11) | copy-start | bytes 196612
  69.4 136.1 %copy-start.4 = (bf16[4,2,4,128]{3,2,1,0:T(4,128)(2,1)S(1)}, bf16[4,2,4,128]{3,2,1,0:T(4,128)(2,1)}, u32[]{:S(2)}) copy-start(bf16[4,2,4,128]{3,2,1,0:T(4,128)(2,1)} %param.13) | copy-start | bytes 24580
  72.5 3.2 copy-start.1
  87.9 3.2 copy-start.1
  103.3 3.2 copy-start.1
  118.7 3.2 copy-start.1
  131.8 11.7 %all-to-all-start.2 = ((bf16[16,2,128]{2,1,0:T(2,128)(2,1)}), bf16[16,2,128]{2,1,0:T(2,128)(2,1)S(1)}, u32[]{:S(2)}, u32[]{:S(2)}) async-start(bf16[16,2,128]{2,1,0:T(2,128)(2,1)} %reshape.228), calls=%async_computation.2 | async-start | bytes 16384 | tf_op jit(solution)/shard_map/all_to_all | solution.py:149
  153.4 95.1 %all-to-all-start = ((bf16[4,32,1,32,128]{4,3,0,2,1:T(8,128)(2,1)}), bf16[4,32,1,32,128]{4,3,0,2,1:T(8,128)(2,1)S(1)}, u32[]{:S(2)}, u32[]{:S(2)}) async-start(bf16[4,32,1,32,128]{4,3,0,2,1:T(8,128)(2,1)} %bitcast.156), calls=%async_computation | async-start | bytes 2097152 | tf_op jit(solution)/shard_map/all_to_all | solution.py:135
  157.0 148.5 %all-gather.5.cloned.1.call-start = ((), (), s32[]{:S(2)}) async-start(), calls=%async_computation.5 | async-start | bytes 1114112 | tf_op jit(solution)/shard_map/all_gather | solution.py:166
  254.4 62.1 %reduce-scatter.2.cloned.1.call-start = ((), (), s32[]{:S(2)}) async-start(), calls=%async_computation.6 | async-start | bytes 196608 | tf_op jit(solution)/shard_map/reduce_scatter | solution.py:170
Sparse Core Ops, SparseCore 0:
  10.1 57.6 all-gather.2
  254.5 50.9 all-gather.4
  310.0 6.4 reduce-scatter.1
where the time goes:
time: 324 us; the launch traced here: 323 us
  blocking collectives  95.6 us (30%)
  waiting for transfers between devices  88.1 us (27%)
  local copies, waits for them, and re-layouts  47.6 us (15%)
  matrix products  39.7 us (12%)
  other arithmetic  30.1 us (9%)
  between operations  13.4 us (4%)
  starting transfers between devices  8.24 us (3%)
    all_gather x1, waiting for transfers between devices, on_device(): lax.all_gather(attention, 'ctx', axis=1, tiled=True)  51.1 us
    all_gather x1, blocking collectives, on_device(): lax.all_gather(cand_keys, 'ctx', axis=1, tiled=True)  47.7 us
    all_gather x1, blocking collectives, on_device(): lax.all_gather(candidate_values, 'ctx', axis=1, tiled=True)  38.1 us
    dot_general x4, matrix products, block_terms(): jnp.einsum('kgnm,mkd->nkgd', weights.astype(jnp.bfloat16), block_values,...  22.9 us
    all_gather x1, waiting for transfers between devices, on_device(): shard_rows = lax.all_gather(queries, 'ctx', axis=1, tiled=True)  22.6 us
    select_n x1, other arithmetic, on_device(): jnp.take(cached_prompt_keys, local_index, axis=0)  14.7 us
    while x8, local copies, waits for them, and re-layouts  12.9 us
    dot_general x4, matrix products, block_terms(): jnp.einsum('nkgd,mkd->kgnm', query_matrix, block_keys, preferred_element_...  12 us
  transfers between devices with their start and end apart: 5, of which 4 were waited for; matrix products, arithmetic and copies ran while one was open for 13% of the time, Pallas kernels for 0%

commit v1 on v0

--- a/solution.py
+++ b/solution.py
@@ -161,12 +161,23 @@
         .reshape(cand_count, tok_rows, head_local * head_size)
         .astype(jnp.bfloat16)
     )
-    partial_value = jnp.einsum(
-        "jnf,fc->jnc",
-        lax.all_gather(attention, "ctx", axis=1, tiled=True),
-        out_weight,
-        preferred_element_type=jnp.float32,
-    )
+    ways, here, turn = (lax.axis_size("ctx"), lax.axis_index("ctx"), attention.shape[1])
+    earlier, later = ([], [])
+    going_up = going_down = attention
+    for far in range(ways // 2 + 1):
+        earlier.append(
+            jnp.einsum("jnf,fc->jnc", going_up, out_weight, preferred_element_type=jnp.float32)
+        )
+        if 0 < far < ways - ways // 2:
+            later.append(
+                jnp.einsum(
+                    "jnf,fc->jnc", going_down, out_weight, preferred_element_type=jnp.float32
+                )
+            )
+        going_up = lax.ppermute(going_up, "ctx", [(d, (d + 1) % ways) for d in range(ways)])
+        going_down = lax.ppermute(going_down, "ctx", [(d, (d - 1) % ways) for d in range(ways)])
+    line = jnp.concatenate([*earlier[::-1], *later], axis=1)
+    partial_value = jnp.roll(line, (here - ways // 2) * earlier[0].shape[1], axis=1)
     return lax.psum_scatter(
         partial_value.astype(jnp.bfloat16), "tp", scatter_dimension=1, tiled=True
     )

time: 324 us -> 344 us (1.062)
  starting transfers between devices: 8.24 us -> 47.8 us
  waiting for transfers between devices: 88.1 us -> 66.7 us
  matrix products: 39.7 us -> 48.6 us
  local copies, waits for them, and re-layouts: 47.6 us -> 40.3 us
    all_gather x1 -> x0, waiting for transfers between devices: 51.1 us -> none  [on_device(): lax.all_gather(attention, 'ctx', axis=1, tiled=True)]
    ppermute x0 -> x15, starting transfers between devices: none -> 39.6 us  [the longest x7 39.3 us: on_device(): lax.ppermute(going_down, 'ctx', [(d, (d - 1) % ways) for d in range(ways)])]
    ppermute x0 -> x15, waiting for transfers between devices: none -> 23.6 us  [the longest x8 23.6 us: on_device(): lax.ppermute(going_up, 'ctx', [(d, (d + 1) % ways) for d in range(ways)])]
    unnamed x3, waiting for transfers between devices: 0.74 us -> 13.4 us
    dot_general x1 -> x16, matrix products: 4.37 us -> 13.3 us  [the longest x9 8.45 us: on_device(): jnp.einsum('jnf,fc->jnc', going_up, out_weight, preferred_element_type=jn...]
    while x8, local copies, waits for them, and re-layouts: 12.9 us -> 4.18 us
    reduce_scatter x1 -> x0, waiting for transfers between devices: 6.57 us -> none  [on_device(): lax.psum_scatter(partial_value.astype(jnp.bfloat16), 'tp', scatter_dimens...]
  transfers between devices with their start and end apart: 5 -> 19, of which waited for: 4 -> 11; matrix products, arithmetic and copies ran while one was open for 13% -> 16% of each run, Pallas kernels for 0% -> 0%
where the time goes in v1:
time: 344 us; the launch traced here: 343 us
  blocking collectives  95.6 us (28%)
  waiting for transfers between devices  66.7 us (19%)
  matrix products  48.6 us (14%)
  starting transfers between devices  47.8 us (14%)
  local copies, waits for them, and re-layouts  40.3 us (12%)
  other arithmetic  29.4 us (9%)
  between operations  14.6 us (4%)
    all_gather x1, blocking collectives, on_device(): lax.all_gather(cand_keys, 'ctx', axis=1, tiled=True)  47.7 us
    ppermute x7, starting transfers between devices, on_device(): lax.ppermute(going_down, 'ctx', [(d, (d - 1) % ways) for d in range(ways)])  39.3 us
    all_gather x1, blocking collectives, on_device(): lax.all_gather(candidate_values, 'ctx', axis=1, tiled=True)  38.1 us
    ppermute x8, waiting for transfers between devices, on_device(): lax.ppermute(going_up, 'ctx', [(d, (d + 1) % ways) for d in range(ways)])  23.6 us
    dot_general x4, matrix products, block_terms(): jnp.einsum('kgnm,mkd->nkgd', weights.astype(jnp.bfloat16), block_values,...  22.8 us
    all_gather x1, waiting for transfers between devices, on_device(): shard_rows = lax.all_gather(queries, 'ctx', axis=1, tiled=True)  22.6 us
    select_n x1, other arithmetic, on_device(): jnp.take(cached_prompt_keys, local_index, axis=0)  14.7 us
    unnamed x3, waiting for transfers between devices  13.4 us
  transfers between devices with their start and end apart: 19, of which 11 were waited for; matrix products, arithmetic and copies ran while one was open for 16% of the time, Pallas kernels for 0%

profile of v1, /device:TPU:0, one launch (start us, length us, event | category | flops | bytes accessed | tf_op | source)
XLA Modules:
  0.0 343.3 jit_solution(12627621155889285662)
XLA Ops:
  10.1 9.3 %gather_fusion.1 = bf16[64,128,4,128]{3,2,1,0:T(4,128)(2,1)} fusion(bf16[16,128,4,128]{3,2,1,0:T(4,128)(2,1)S(1)} %copy-done, s32[1024]{0:T(1024)S(1)} %pad_clamp_fusion), kind=kCustom, calls=%fused_computation.clone | custom fusion | bytes 16777472 | tf_op jit(solution)/shard_map/jit(_take)/gather | solution.py:91
  19.4 11.0 %gather_fusion.2 = bf16[64,128,4,128]{3,2,1,0:T(4,128)(2,1)} fusion(bf16[16,128,4,128]{3,2,1,0:T(4,128)(2,1)} %param.14, s32[1024]{0:T(1024)S(1)} %pad_clamp_fusion), kind=kCustom, calls=%fused_computation.1.clone | custom fusion | bytes 16777472 | tf_op jit(solution)/shard_map/jit(_take)/gather | solution.py:88
  30.5 14.7 %copy_select_fusion = (bf16[4,16,128,4,128]{4,2,1,3,0:T(8,128)(2,1)}, bf16[4,16,128,4,128]{4,2,1,3,0:T(8,128)(2,1)}) fusion(bf16[4,16,128,4,128]{4,3,2,1,0:T(4,128)(2,1)} %bitcast.231, pred[4,16]{1,0:T(4,128)(4,1)S(1)} %get-tuple-element.82, bf16[4,16,128,4,128]{4,3,2,1,0:T(4,128)(2,1)} %bitcast.230), kind=kLoop, calls=%fused_computation.27 | loop fusion | flops 8388608 | bytes 33554496 | tf_op jit(solution)/shard_map/jit(_take)/select_n | solution.py:88
  45.2 22.6 %all-gather.2.cloned.1.call-done = bf16[4,32,32,128]{3,2,1,0:T(8,128)(2,1)} async-done(((bf16[4,2,32,128]{3,2,1,0:T(8,128)(2,1)}), bf16[4,32,32,128]{3,2,1,0:T(8,128)(2,1)}) %all-gather.2.cloned.1.call-update) | async-done | bytes 1048592 | tf_op jit(solution)/shard_map/all_gather | solution.py:95
  69.4 52.8 %while.14 = (s32[]{:T(128)}, bf16[4,32,32,128]{3,2,0,1:T(8,128)(2,1)}, bf16[4,32,32]{2,0,1:T(4,128)(2,1)S(1)}, bf16[4,32,32]{2,0,1:T(4,128)(2,1)S(1)}, bf16[4,20...) while((s32[]{:T(128)}, ...), condition=%wide.region_5.7_spmd, body=%wide.region_2.6_spmd.sunk | while | flops 1101002752 | bytes 64022668 | solution.py:100
  75.9 5.7 %fusion.99 = bf16[4,128,8,32]{1,3,2,0:T(8,128)(2,1)S(1)} fusion(f32[4,2048,32,8]{1,2,3,0:T(8,128)} %copy-done.2, f32[4,8,32]{2,1,0:T(8,128)S(1)} %get-tuple-element.180, pred[2048]{0:T(1024)(128)(4,1)S(1)} %dynamic-slice_reduce_fusion.2, bf16[4,2048,4,128]{3,1,2,0:T(8,128)(2,1)} %get-tuple-element.205, s32[]{:T(128)} %get-tuple-element.191), kind=kOutput, calls=%fused_computation.10.clone.1 | convolution fusion | flops 547356672 | bytes 10768896 | tf_op jit(solution)/shard_map/while/body/eval_jaxpr/kgnm,mkd->nkgd/dot_general | solution.py:28
  89.1 5.7 %fusion.99 = bf16[4,128,8,32]{1,3,2,0:T(8,128)(2,1)S(1)} fusion(f32[4,2048,32,8]{1,2,3,0:T(8,128)} %copy-done.2, f32[4,8,32]{2,1,0:T(8,128)S(1)} %get-tuple-element.180, pred[2048]{0:T(1024)(128)(4,1)S(1)} %dynamic-slice_reduce_fusion.2, bf16[4,2048,4,128]{3,1,2,0:T(8,128)(2,1)} %get-tuple-element.205, s32[]{:T(128)} %get-tuple-element.191), kind=kOutput, calls=%fused_computation.10.clone.1 | convolution fusion | flops 547356672 | bytes 10768896 | tf_op jit(solution)/shard_map/while/body/eval_jaxpr/kgnm,mkd->nkgd/dot_general | solution.py:28
  102.3 5.7 %fusion.99 = bf16[4,128,8,32]{1,3,2,0:T(8,128)(2,1)S(1)} fusion(f32[4,2048,32,8]{1,2,3,0:T(8,128)} %copy-done.2, f32[4,8,32]{2,1,0:T(8,128)S(1)} %get-tuple-element.180, pred[2048]{0:T(1024)(128)(4,1)S(1)} %dynamic-slice_reduce_fusion.2, bf16[4,2048,4,128]{3,1,2,0:T(8,128)(2,1)} %get-tuple-element.205, s32[]{:T(128)} %get-tuple-element.191), kind=kOutput, calls=%fused_computation.10.clone.1 | convolution fusion | flops 547356672 | bytes 10768896 | tf_op jit(solution)/shard_map/while/body/eval_jaxpr/kgnm,mkd->nkgd/dot_general | solution.py:28
  115.5 5.7 %fusion.99 = bf16[4,128,8,32]{1,3,2,0:T(8,128)(2,1)S(1)} fusion(f32[4,2048,32,8]{1,2,3,0:T(8,128)} %copy-done.2, f32[4,8,32]{2,1,0:T(8,128)S(1)} %get-tuple-element.180, pred[2048]{0:T(1024)(128)(4,1)S(1)} %dynamic-slice_reduce_fusion.2, bf16[4,2048,4,128]{3,1,2,0:T(8,128)(2,1)} %get-tuple-element.205, s32[]{:T(128)} %get-tuple-element.191), kind=kOutput, calls=%fused_computation.10.clone.1 | convolution fusion | flops 547356672 | bytes 10768896 | tf_op jit(solution)/shard_map/while/body/eval_jaxpr/kgnm,mkd->nkgd/dot_general | solution.py:28
  123.0 4.5 %all-to-all-start.2 = ((bf16[16,2,128]{2,1,0:T(2,128)(2,1)}), bf16[16,2,128]{2,1,0:T(2,128)(2,1)S(1)}, u32[]{:S(2)}, u32[]{:S(2)}) async-start(bf16[16,2,128]{2,1,0:T(2,128)(2,1)} %reshape.230), calls=%async_computation.2 | async-start | bytes 16384 | tf_op jit(solution)/shard_map/all_to_all | solution.py:149
  127.6 7.1 %all-to-all-done.2 = bf16[16,2,128]{2,1,0:T(2,128)(2,1)S(1)} async-done(((bf16[16,2,128]{2,1,0:T(2,128)(2,1)}), bf16[16,2,128]{2,1,0:T(2,128)(2,1)S(1)}, u32[]{:S(2)}, u32[]{:S(2)}) %all-to-all-start.2) | async-done | bytes 8224 | tf_op jit(solution)/shard_map/all_to_all | solution.py:149
  134.7 9.9 %all_to_all.33 = bf16[16,2,128]{2,1,0:T(2,128)(2,1)S(1)} all-to-all(bf16[16,2,128]{2,1,0:T(2,128)(2,1)S(1)} %reshape.228), channel_id=1, replica_groups=mesh['groups'=1,'ctx'=16,'tp'=2] {'ctx'}, dimensions={0} | all-to-all | bytes 16384 | tf_op jit(solution)/shard_map/all_to_all | solution.py:142
  148.3 47.7 %all_gather.10 = bf16[4,32,4,128]{3,2,0,1:T(4,128)(2,1)S(1)} all-gather(bf16[4,2,4,128]{3,2,0,1:T(4,128)(2,1)S(1)} %copy.90), channel_id=1, replica_groups=mesh['groups'=1,'ctx'=16,'tp'=2] {'ctx'}, dimensions={1}, use_global_device_ids=true | all-gather | bytes 139264 | tf_op jit(solution)/shard_map/all_gather | solution.py:106
  196.8 38.1 %all_gather.11 = bf16[4,32,4,128]{3,2,0,1:T(4,128)(2,1)S(1)} all-gather(bf16[4,2,4,128]{3,2,0,1:T(4,128)(2,1)S(1)} %copy.96), channel_id=1, replica_groups=mesh['groups'=1,'ctx'=16,'tp'=2] {'ctx'}, dimensions={1}, use_global_device_ids=true | all-gather | bytes 139264 | tf_op jit(solution)/shard_map/all_gather | solution.py:107
  239.0 3.9 %fusion.52 = f32[4,2,32,128]{3,1,2,0:T(2,128)S(1)} fusion(f32[4,16,2,1,32,128]{5,4,0,2,1,3:T(8,128)S(1)} %convert.23, f32[4,2,16,32]{1,2,3,0:T(8,128)} %copy.89), kind=kLoop, calls=%fused_computation.62 | loop fusion | flops 1015808 | bytes 2244608 | tf_op jit(solution)/shard_map/reduce_sum | solution.py:54
  243.6 7.7 %collective-permute-done = bf16[4,2,4096]{2,0,1:T(4,128)(2,1)S(1)} collective-permute-done((bf16[4,2,4096]{2,0,1:T(4,128)(2,1)S(1)}, bf16[4,2,4096]{2,0,1:T(4,128)(2,1)S(1)}, u32[]{:S(2)}, u32[]{:S(2)}) %collective-permute-start) | collective-permute-done | bytes 65568 | tf_op jit(solution)/shard_map/ppermute | solution.py:177
  251.3 5.6 %collective-permute-start.8 = (bf16[4,2,4096]{2,0,1:T(4,128)(2,1)S(1)}, bf16[4,2,4096]{2,0,1:T(4,128)(2,1)S(1)}, u32[]{:S(2)}, u32[]{:S(2)}) collective-permute-start(bf16[4,2,4096]{2,0,1:T(4,128)(2,1)S(1)} %fusion.57), channel_id=1, source_target_pairs={{0,30},{2,0},{4,2},{6,4},{8,6},{10,8},{12,10},{14,12},{16,14},{18,... | collective-permute-start | bytes 196616 | tf_op jit(solution)/shard_map/ppermute | solution.py:178
  259.4 5.6 %collective-permute-start.9 = (bf16[4,2,4096]{2,0,1:T(4,128)(2,1)S(1)}, bf16[4,2,4096]{2,0,1:T(4,128)(2,1)S(1)}, u32[]{:S(2)}, u32[]{:S(2)}) collective-permute-start(bf16[4,2,4096]{2,0,1:T(4,128)(2,1)S(1)} %collective-permute-done.8), channel_id=1, source_target_pairs={{0,30},{2,0},{4,2},{6,4},{8,6},{10,8},{12,10},{14,12},{16,14},{18,... | collective-permute-start | bytes 196616 | tf_op jit(solution)/shard_map/ppermute | solution.py:178
  267.3 5.6 %collective-permute-start.10 = (bf16[4,2,4096]{2,0,1:T(4,128)(2,1)S(1)}, bf16[4,2,4096]{2,0,1:T(4,128)(2,1)S(1)}, u32[]{:S(2)}, u32[]{:S(2)}) collective-permute-start(bf16[4,2,4096]{2,0,1:T(4,128)(2,1)S(1)} %collective-permute-done.9), channel_id=1, source_target_pairs={{0,30},{2,0},{4,2},{6,4},{8,6},{10,8},{12,10},{14,12},{16,14},{18,... | collective-permute-start | bytes 196616 | tf_op jit(solution)/shard_map/ppermute | solution.py:178
  275.1 5.6 %collective-permute-start.11 = (bf16[4,2,4096]{2,0,1:T(4,128)(2,1)S(1)}, bf16[4,2,4096]{2,0,1:T(4,128)(2,1)S(1)}, u32[]{:S(2)}, u32[]{:S(2)}) collective-permute-start(bf16[4,2,4096]{2,0,1:T(4,128)(2,1)S(1)} %collective-permute-done.10), channel_id=1, source_target_pairs={{0,30},{2,0},{4,2},{6,4},{8,6},{10,8},{12,10},{14,12},{16,14},{18,... | collective-permute-start | bytes 196616 | tf_op jit(solution)/shard_map/ppermute | solution.py:178
  283.0 5.6 %collective-permute-start.12 = (bf16[4,2,4096]{2,0,1:T(4,128)(2,1)S(1)}, bf16[4,2,4096]{2,0,1:T(4,128)(2,1)S(1)}, u32[]{:S(2)}, u32[]{:S(2)}) collective-permute-start(bf16[4,2,4096]{2,0,1:T(4,128)(2,1)S(1)} %collective-permute-done.11), channel_id=1, source_target_pairs={{0,30},{2,0},{4,2},{6,4},{8,6},{10,8},{12,10},{14,12},{16,14},{18,... | collective-permute-start | bytes 196616 | tf_op jit(solution)/shard_map/ppermute | solution.py:178
  290.9 5.6 %collective-permute-start.13 = (bf16[4,2,4096]{2,0,1:T(4,128)(2,1)S(1)}, bf16[4,2,4096]{2,0,1:T(4,128)(2,1)S(1)}, u32[]{:S(2)}, u32[]{:S(2)}) collective-permute-start(bf16[4,2,4096]{2,0,1:T(4,128)(2,1)S(1)} %collective-permute-done.12), channel_id=1, source_target_pairs={{0,30},{2,0},{4,2},{6,4},{8,6},{10,8},{12,10},{14,12},{16,14},{18,... | collective-permute-start | bytes 196616 | tf_op jit(solution)/shard_map/ppermute | solution.py:178
  298.7 5.6 %collective-permute-start.14 = (bf16[4,2,4096]{2,0,1:T(4,128)(2,1)S(1)}, bf16[4,2,4096]{2,0,1:T(4,128)(2,1)S(1)}, u32[]{:S(2)}, u32[]{:S(2)}) collective-permute-start(bf16[4,2,4096]{2,0,1:T(4,128)(2,1)S(1)} %collective-permute-done.13), channel_id=1, source_target_pairs={{0,30},{2,0},{4,2},{6,4},{8,6},{10,8},{12,10},{14,12},{16,14},{18,... | collective-permute-start | bytes 196616 | tf_op jit(solution)/shard_map/ppermute | solution.py:178
  322.3 12.7 %all-reduce.3.cloned.1.call-done = bf16[4,32,512]{2,0,1:T(4,128)(2,1)} async-done(((bf16[4,32,512]{2,0,1:T(4,128)(2,1)}), bf16[4,32,512]{2,0,1:T(4,128)(2,1)}) %all-reduce.3.cloned.1.call-update) | async-done | bytes 131088
  (173 shorter events, 77.3 us)
Async XLA Ops:
  6.5 61.2 %all-gather.2.cloned.1.call-start = ((), (), s32[]{:S(2)}) async-start(), calls=%async_computation.3 | async-start | bytes 1114112 | tf_op jit(solution)/shard_map/all_gather | solution.py:95
  69.4 78.9 %copy-start.6 = (bf16[4,2,4,128]{3,2,1,0:T(4,128)(2,1)S(1)}, bf16[4,2,4,128]{3,2,1,0:T(4,128)(2,1)}, u32[]{:S(2)}) copy-start(bf16[4,2,4,128]{3,2,1,0:T(4,128)(2,1)} %param.12) | copy-start | bytes 24580
  69.4 126.7 %copy-start.5 = (bf16[4,2,32,128]{3,2,1,0:T(8,128)(2,1)S(1)}, bf16[4,2,32,128]{3,2,1,0:T(8,128)(2,1)}, u32[]{:S(2)}) copy-start(bf16[4,2,32,128]{3,2,1,0:T(8,128)(2,1)} %param.11) | copy-start | bytes 196612
  69.4 127.4 %copy-start.7 = (bf16[4,2,4,128]{3,2,1,0:T(4,128)(2,1)S(1)}, bf16[4,2,4,128]{3,2,1,0:T(4,128)(2,1)}, u32[]{:S(2)}) copy-start(bf16[4,2,4,128]{3,2,1,0:T(4,128)(2,1)} %param.13) | copy-start | bytes 24580
  123.0 11.7 %all-to-all-start.2 = ((bf16[16,2,128]{2,1,0:T(2,128)(2,1)}), bf16[16,2,128]{2,1,0:T(2,128)(2,1)S(1)}, u32[]{:S(2)}, u32[]{:S(2)}) async-start(bf16[16,2,128]{2,1,0:T(2,128)(2,1)} %reshape.230), calls=%async_computation.2 | async-start | bytes 16384 | tf_op jit(solution)/shard_map/all_to_all | solution.py:149
  144.6 94.1 %all-to-all-start = ((bf16[4,32,1,32,128]{4,3,0,2,1:T(8,128)(2,1)}), bf16[4,32,1,32,128]{4,3,0,2,1:T(8,128)(2,1)S(1)}, u32[]{:S(2)}, u32[]{:S(2)}) async-start(bf16[4,32,1,32,128]{4,3,0,2,1:T(8,128)(2,1)} %bitcast.237), calls=%async_computation | async-start | bytes 2097152 | tf_op jit(solution)/shard_map/all_to_all | solution.py:135
  148.2 186.7 %all-reduce.3.cloned.1.call-start = ((), (), s32[]{:S(2)}) async-start(), calls=%async_computation.4 | async-start | bytes 262144
  238.7 4.5 %copy-start.3 = (f32[4,2,4096]{2,0,1:T(4,128)S(1)}, f32[4,2,4096]{2,0,1:T(4,128)}, u32[]{:S(2)}) copy-start(f32[4,2,4096]{2,0,1:T(4,128)} %mul.81) | copy-start | bytes 393220
  243.3 8.0 %collective-permute-start = (bf16[4,2,4096]{2,0,1:T(4,128)(2,1)S(1)}, bf16[4,2,4096]{2,0,1:T(4,128)(2,1)S(1)}, u32[]{:S(2)}, u32[]{:S(2)}) collective-permute-start(bf16[4,2,4096]{2,0,1:T(4,128)(2,1)S(1)} %fusion.57), channel_id=1, source_target_pairs={{0,2},{2,4},{4,6},{6,8},{8,10},{10,12},{12,14},{14,16},{16,18},{18... | collective-permute-start | bytes 196616 | tf_op jit(solution)/shard_map/ppermute | solution.py:177
  251.3 8.1 %collective-permute-start.1 = (bf16[4,2,4096]{2,0,1:T(4,128)(2,1)S(1)}, bf16[4,2,4096]{2,0,1:T(4,128)(2,1)S(1)}, u32[]{:S(2)}, u32[]{:S(2)}) collective-permute-start(bf16[4,2,4096]{2,0,1:T(4,128)(2,1)S(1)} %collective-permute-done), channel_id=1, source_target_pairs={{0,2},{2,4},{4,6},{6,8},{8,10},{10,12},{12,14},{14,16},{16,18},{18... | collective-permute-start | bytes 196616 | tf_op jit(solution)/shard_map/ppermute | solution.py:177
  251.3 8.1 %collective-permute-start.8 = (bf16[4,2,4096]{2,0,1:T(4,128)(2,1)S(1)}, bf16[4,2,4096]{2,0,1:T(4,128)(2,1)S(1)}, u32[]{:S(2)}, u32[]{:S(2)}) collective-permute-start(bf16[4,2,4096]{2,0,1:T(4,128)(2,1)S(1)} %fusion.57), channel_id=1, source_target_pairs={{0,30},{2,0},{4,2},{6,4},{8,6},{10,8},{12,10},{14,12},{16,14},{18,... | collective-permute-start | bytes 196616 | tf_op jit(solution)/shard_map/ppermute | solution.py:178
  259.4 7.9 %collective-permute-start.2 = (bf16[4,2,4096]{2,0,1:T(4,128)(2,1)S(1)}, bf16[4,2,4096]{2,0,1:T(4,128)(2,1)S(1)}, u32[]{:S(2)}, u32[]{:S(2)}) collective-permute-start(bf16[4,2,4096]{2,0,1:T(4,128)(2,1)S(1)} %collective-permute-done.1), channel_id=1, source_target_pairs={{0,2},{2,4},{4,6},{6,8},{8,10},{10,12},{12,14},{14,16},{16,18},{18... | collective-permute-start | bytes 196616 | tf_op jit(solution)/shard_map/ppermute | solution.py:177
  259.4 7.9 %collective-permute-start.9 = (bf16[4,2,4096]{2,0,1:T(4,128)(2,1)S(1)}, bf16[4,2,4096]{2,0,1:T(4,128)(2,1)S(1)}, u32[]{:S(2)}, u32[]{:S(2)}) collective-permute-start(bf16[4,2,4096]{2,0,1:T(4,128)(2,1)S(1)} %collective-permute-done.8), channel_id=1, source_target_pairs={{0,30},{2,0},{4,2},{6,4},{8,6},{10,8},{12,10},{14,12},{16,14},{18,... | collective-permute-start | bytes 196616 | tf_op jit(solution)/shard_map/ppermute | solution.py:178
  267.3 7.9 %collective-permute-start.3 = (bf16[4,2,4096]{2,0,1:T(4,128)(2,1)S(1)}, bf16[4,2,4096]{2,0,1:T(4,128)(2,1)S(1)}, u32[]{:S(2)}, u32[]{:S(2)}) collective-permute-start(bf16[4,2,4096]{2,0,1:T(4,128)(2,1)S(1)} %collective-permute-done.2), channel_id=1, source_target_pairs={{0,2},{2,4},{4,6},{6,8},{8,10},{10,12},{12,14},{14,16},{16,18},{18... | collective-permute-start | bytes 196616 | tf_op jit(solution)/shard_map/ppermute | solution.py:177
  267.3 7.9 %collective-permute-start.10 = (bf16[4,2,4096]{2,0,1:T(4,128)(2,1)S(1)}, bf16[4,2,4096]{2,0,1:T(4,128)(2,1)S(1)}, u32[]{:S(2)}, u32[]{:S(2)}) collective-permute-start(bf16[4,2,4096]{2,0,1:T(4,128)(2,1)S(1)} %collective-permute-done.9), channel_id=1, source_target_pairs={{0,30},{2,0},{4,2},{6,4},{8,6},{10,8},{12,10},{14,12},{16,14},{18,... | collective-permute-start | bytes 196616 | tf_op jit(solution)/shard_map/ppermute | solution.py:178
  275.1 7.9 %collective-permute-start.4 = (bf16[4,2,4096]{2,0,1:T(4,128)(2,1)S(1)}, bf16[4,2,4096]{2,0,1:T(4,128)(2,1)S(1)}, u32[]{:S(2)}, u32[]{:S(2)}) collective-permute-start(bf16[4,2,4096]{2,0,1:T(4,128)(2,1)S(1)} %collective-permute-done.3), channel_id=1, source_target_pairs={{0,2},{2,4},{4,6},{6,8},{8,10},{10,12},{12,14},{14,16},{16,18},{18... | collective-permute-start | bytes 196616 | tf_op jit(solution)/shard_map/ppermute | solution.py:177
  275.1 7.9 %collective-permute-start.11 = (bf16[4,2,4096]{2,0,1:T(4,128)(2,1)S(1)}, bf16[4,2,4096]{2,0,1:T(4,128)(2,1)S(1)}, u32[]{:S(2)}, u32[]{:S(2)}) collective-permute-start(bf16[4,2,4096]{2,0,1:T(4,128)(2,1)S(1)} %collective-permute-done.10), channel_id=1, source_target_pairs={{0,30},{2,0},{4,2},{6,4},{8,6},{10,8},{12,10},{14,12},{16,14},{18,... | collective-permute-start | bytes 196616 | tf_op jit(solution)/shard_map/ppermute | solution.py:178
  283.0 7.9 %collective-permute-start.5 = (bf16[4,2,4096]{2,0,1:T(4,128)(2,1)S(1)}, bf16[4,2,4096]{2,0,1:T(4,128)(2,1)S(1)}, u32[]{:S(2)}, u32[]{:S(2)}) collective-permute-start(bf16[4,2,4096]{2,0,1:T(4,128)(2,1)S(1)} %collective-permute-done.4), channel_id=1, source_target_pairs={{0,2},{2,4},{4,6},{6,8},{8,10},{10,12},{12,14},{14,16},{16,18},{18... | collective-permute-start | bytes 196616 | tf_op jit(solution)/shard_map/ppermute | solution.py:177
  283.0 7.9 %collective-permute-start.12 = (bf16[4,2,4096]{2,0,1:T(4,128)(2,1)S(1)}, bf16[4,2,4096]{2,0,1:T(4,128)(2,1)S(1)}, u32[]{:S(2)}, u32[]{:S(2)}) collective-permute-start(bf16[4,2,4096]{2,0,1:T(4,128)(2,1)S(1)} %collective-permute-done.11), channel_id=1, source_target_pairs={{0,30},{2,0},{4,2},{6,4},{8,6},{10,8},{12,10},{14,12},{16,14},{18,... | collective-permute-start | bytes 196616 | tf_op jit(solution)/shard_map/ppermute | solution.py:178
  290.9 7.9 %collective-permute-start.6 = (bf16[4,2,4096]{2,0,1:T(4,128)(2,1)S(1)}, bf16[4,2,4096]{2,0,1:T(4,128)(2,1)S(1)}, u32[]{:S(2)}, u32[]{:S(2)}) collective-permute-start(bf16[4,2,4096]{2,0,1:T(4,128)(2,1)S(1)} %collective-permute-done.5), channel_id=1, source_target_pairs={{0,2},{2,4},{4,6},{6,8},{8,10},{10,12},{12,14},{14,16},{16,18},{18... | collective-permute-start | bytes 196616 | tf_op jit(solution)/shard_map/ppermute | solution.py:177
  290.9 7.9 %collective-permute-start.13 = (bf16[4,2,4096]{2,0,1:T(4,128)(2,1)S(1)}, bf16[4,2,4096]{2,0,1:T(4,128)(2,1)S(1)}, u32[]{:S(2)}, u32[]{:S(2)}) collective-permute-start(bf16[4,2,4096]{2,0,1:T(4,128)(2,1)S(1)} %collective-permute-done.12), channel_id=1, source_target_pairs={{0,30},{2,0},{4,2},{6,4},{8,6},{10,8},{12,10},{14,12},{16,14},{18,... | collective-permute-start | bytes 196616 | tf_op jit(solution)/shard_map/ppermute | solution.py:178
  298.7 7.9 %collective-permute-start.7 = (bf16[4,2,4096]{2,0,1:T(4,128)(2,1)S(1)}, bf16[4,2,4096]{2,0,1:T(4,128)(2,1)S(1)}, u32[]{:S(2)}, u32[]{:S(2)}) collective-permute-start(bf16[4,2,4096]{2,0,1:T(4,128)(2,1)S(1)} %collective-permute-done.6), channel_id=1, source_target_pairs={{0,2},{2,4},{4,6},{6,8},{8,10},{10,12},{12,14},{14,16},{16,18},{18... | collective-permute-start | bytes 196616 | tf_op jit(solution)/shard_map/ppermute | solution.py:177
  298.7 10.7 %copy-start.1 = (bf16[4096,512]{1,0:T(8,128)(2,1)S(1)}, bf16[4096,512]{1,0:T(8,128)(2,1)}, u32[]{:S(2)}) copy-start(bf16[4096,512]{1,0:T(8,128)(2,1)} %param.17) | copy-start | bytes 12582916
  298.7 20.6 %collective-permute-start.14 = (bf16[4,2,4096]{2,0,1:T(4,128)(2,1)S(1)}, bf16[4,2,4096]{2,0,1:T(4,128)(2,1)S(1)}, u32[]{:S(2)}, u32[]{:S(2)}) collective-permute-start(bf16[4,2,4096]{2,0,1:T(4,128)(2,1)S(1)} %collective-permute-done.13), channel_id=1, source_target_pairs={{0,30},{2,0},{4,2},{6,4},{8,6},{10,8},{12,10},{14,12},{16,14},{18,... | collective-permute-start | bytes 196616 | tf_op jit(solution)/shard_map/ppermute | solution.py:178
  (7 other events, 22.6 us)
Sparse Core Ops, SparseCore 0:
  10.1 57.6 all-gather.1
  321.1 13.7 all-reduce.2
